TPU v7x, 32 devices: a whole 2x2x4 slice. The times are simulated.
32 devices in a mesh: groups: 2 (over x), width: 16 (over z, y, core).
Axes of the slice: x: 2, y: 2, z: 4, core: 2. Of those that a mesh axis runs over, the one named last changes fastest.
Arguments:
- stream_in: bfloat16 [2, 128, 8192], P(None, 'groups', 'width'), parts along dimension 1, may hold values from -16 to 16
- norm_gain: float32 [2, 8192], replicated, may hold values from 0.1 to 1.9
- w_gate: bfloat16 [2, 8192, 14336], P(None, None, 'width'), may hold values from -0.0625 to 0.0625
- w_up: bfloat16 [2, 8192, 14336], P(None, None, 'width'), may hold values from -0.0625 to 0.0625
- w_down: bfloat16 [2, 14336, 8192], P(None, 'width'), may hold values from -0.0625 to 0.0625
Outputs:
- stream_out: bfloat16 [2, 128, 8192], P(None, 'groups', 'width'), parts along dimension 1
There are 2 independent parts, one for each index of `groups`. A program takes and returns all parts, laid end to end along the dimension named above; an argument that names none is the same for every part. Nothing has to cross between parts.
All inputs are finite; a program needn't handle non-finite values.
Results may differ from a plain program's by a relative error of at most 0.012.
Values may be sent and summed in bfloat16 or wider, within the bound.
A program may use at most 192 MiB of HBM per device.

v0:
```python
import jax
import jax.numpy as jnp
from jax import lax
from jax.sharding import PartitionSpec as P

LAYERS = 2
MICRO = 2


def body(stream_in, norm_gain, w_gate, w_up, w_down):
    width_local = stream_in.shape[2]
    offset = lax.axis_index("width") * width_local
    starts = [
        lax.all_gather(stream_in[micro_index], "width", axis=1, tiled=True)
        for micro_index in range(MICRO)
    ]
    results = []
    for micro_index in range(MICRO):
        stream = starts[micro_index]
        for depth in range(LAYERS):
            stream_f = stream.astype(jnp.float32)
            meansq = jnp.mean(stream_f * stream_f, axis=1, keepdims=True)
            normed = (stream_f * lax.rsqrt(meansq + 1e-05) * norm_gain[depth]).astype(jnp.bfloat16)
            gate_out = jnp.dot(normed, w_gate[depth], preferred_element_type=jnp.float32)
            up_out = jnp.dot(normed, w_up[depth], preferred_element_type=jnp.float32)
            hidden = (jax.nn.silu(gate_out) * up_out).astype(jnp.bfloat16)
            partials = jnp.dot(hidden, w_down[depth], preferred_element_type=jnp.float32)
            branch = lax.psum(partials, "width")
            stream = (stream_f + branch).astype(jnp.bfloat16)
        results.append(stream)
    results = [lax.dynamic_slice_in_dim(stream, offset, width_local, 1) for stream in results]
    return jnp.stack(results)


def solution(mesh):
    return jax.shard_map(
        body,
        mesh=mesh,
        in_specs=(
            P(None, "groups", "width"),
            P(),
            P(None, None, "width"),
            P(None, None, "width"),
            P(None, "width", None),
        ),
        out_specs=P(None, "groups", "width"),
        check_vma=False,
    )
```

profile of v0, /device:TPU:0, one launch (start us, length us, event | category | flops | bytes accessed | tf_op | source)
XLA Modules:
  0.0 415.5 jit_solution(16510495588360910265)
XLA Ops:
  6.5 0.0 all-gather.5.cloned.1.call-start
  6.5 1.5 fusion.118
  8.1 0.0 all-gather.5.cloned.1.call-update
  8.1 0.0 all-gather.7.cloned.1.call-start
  8.1 0.7 all-gather.7.cloned.1.call-update
  8.8 0.0 all-reduce.7.cloned.1.call-start
  8.9 1.0 fusion.119
  9.9 39.0 %all-gather.5.cloned.1.call-done = bf16[1,64,8192]{2,1,0:T(8,128)(2,1)} async-done(((bf16[1,64,512]{2,1,0:T(8,128)(2,1)}), bf16[1,64,8192]{2,1,0:T(8,128)(2,1)}) %all-gather.5.cloned.1.call-update) | async-done | bytes 1048592 | tf_op jit(solution)/shard_map/all_gather | solution.py:14
  48.9 1.6 fusion.36
  50.5 36.8 %all-gather.7.cloned.1.call-done = bf16[1,64,8192]{2,1,0:T(8,128)(2,1)} async-done(((bf16[1,64,512]{2,1,0:T(8,128)(2,1)}), bf16[1,64,8192]{2,1,0:T(8,128)(2,1)}) %all-gather.7.cloned.1.call-update) | async-done | bytes 1048592 | tf_op jit(solution)/shard_map/all_gather | solution.py:14
  87.3 1.5 fusion.40
  88.9 0.0 copy-done
  88.9 0.0 copy-start.1
  88.9 6.7 %fusion.22 = f32[64,896]{1,0:T(8,128)S(1)} fusion(bf16[2,8192,896]{2,1,0:T(8,128)(2,1)} %param.7, bf16[1,64,8192]{2,1,0:T(8,128)(2,1)S(1)} %copy-done, f32[8192]{0:T(1024)S(1)} %bitcast.82, f32[64]{0:T(128)S(1)} %add_rsqrt_fusion.3), kind=kOutput, calls=%fused_computation.22 | convolution fusion | flops 941621248 | bytes 15991040 | tf_op jit(solution)/shard_map/dot_general | solution.py:24
  95.6 0.0 copy-done.1
  95.6 6.6 %fusion.20 = f32[64,896]{1,0:T(8,128)S(1)} fusion(bf16[2,8192,896]{2,1,0:T(8,128)(2,1)} %param.7, bf16[1,64,8192]{2,1,0:T(8,128)(2,1)S(1)} %copy-done.1, f32[64]{0:T(128)S(1)} %add_rsqrt_fusion.1, f32[8192]{0:T(1024)S(1)} %bitcast.83), kind=kOutput, calls=%fused_computation.20 | convolution fusion | flops 941621248 | bytes 15991040 | tf_op jit(solution)/shard_map/dot_general | solution.py:24
  102.2 16.4 %fusion.14 = f32[64,8192]{1,0:T(8,128)} fusion(bf16[2,896,8192]{2,1,0:T(8,128)(2,1)} %param.9, bf16[2,8192,896]{2,1,0:T(8,128)(2,1)} %param.8, bf16[1,64,8192]{2,1,0:T(8,128)(2,1)S(1)} %copy-done, f32[8192]{0:T(1024)S(1)} %bitcast.84, f32[64]{0:T(128)S(1)} %add_rsqrt_fusion.3, f32[64,896]{1,0:T(8,128)S(1)} %fusion.22), kind=kOutput, calls=%fused_computation.14 | convolution fusion | flops 1881489408 | bytes 32768256 | tf_op jit(solution)/shard_map/dot_general | solution.py:27
  118.6 16.3 %fusion.12 = f32[64,8192]{1,0:T(8,128)} fusion(bf16[2,896,8192]{2,1,0:T(8,128)(2,1)} %param.9, bf16[2,8192,896]{2,1,0:T(8,128)(2,1)} %param.8, bf16[1,64,8192]{2,1,0:T(8,128)(2,1)S(1)} %copy-done.1, f32[64]{0:T(128)S(1)} %add_rsqrt_fusion.1, f32[8192]{0:T(1024)S(1)} %bitcast.85, f32[64,896]{1,0:T(8,128)S(1)} %fusion.20), kind=kOutput, calls=%fused_computation.12 | convolution fusion | flops 1881489408 | bytes 32768256 | tf_op jit(solution)/shard_map/dot_general | solution.py:27
  134.9 0.0 all-reduce.7.cloned.1.call-update
  134.9 0.2 all-reduce.5.cloned.1.call-start
  135.2 110.9 %all-reduce.7.cloned.1.call-done = (f32[64,8192]{1,0:T(8,128)}, f32[64,8192]{1,0:T(8,128)}) async-done(((f32[64,8192]{1,0:T(8,128)}, f32[64,8192]{1,0:T(8,128)}), (f32[64,8192]{1,0:T(8,128)}, f32[64,8192]{1,0:T(8,128)})) %all-reduce.7.cloned.1.call-update) | async-done | bytes 4194320 | tf_op jit(solution)/shard_map/psum | solution.py:28
  246.0 4.2 %multiply_reduce_fusion = (f32[64]{0:T(128)S(1)}, f32[64,8192]{1,0:T(8,128)}, f32[64]{0:T(128)S(1)}, f32[64,8192]{1,0:T(8,128)S(1)}) fusion(f32[64,8192]{1,0:T(8,128)} %get-tuple-element.7, bf16[1,64,8192]{2,1,0:T(8,128)(2,1)S(1)} %copy-done.1, f32[64,8192]{1,0:T(8,128)} %get-tuple-element.8, bf16[1,64,8192]{2,1,0:T(8,128)(2,1)S(1)} %copy-done), kind=kLoop, calls=%fused_computation.51 | loop fusion | flops 6291328 | bytes 10486272 | tf_op jit(solution)/shard_map/reduce_sum | solution.py:22
  250.2 1.3 copy-done.3
  251.6 6.6 %fusion.10 = f32[64,896]{1,0:T(8,128)S(1)} fusion(bf16[2,8192,896]{2,1,0:T(8,128)(2,1)} %param.7, f32[64,8192]{1,0:T(8,128)S(1)} %get-tuple-element.18, f32[8192]{0:T(1024)S(1)} %bitcast.78, f32[64]{0:T(128)S(1)} %add_rsqrt_fusion.2), kind=kOutput, calls=%fused_computation.10 | convolution fusion | flops 941096960 | bytes 17039616 | tf_op jit(solution)/shard_map/dot_general | solution.py:24
  258.2 14.6 %fusion.2 = f32[64,8192]{1,0:T(8,128)} fusion(bf16[2,896,8192]{2,1,0:T(8,128)(2,1)} %param.9, bf16[2,8192,896]{2,1,0:T(8,128)(2,1)} %param.8, f32[64,896]{1,0:T(8,128)S(1)} %fusion.10, f32[64,8192]{1,0:T(8,128)} %copy-done.3, f32[8192]{0:T(1024)S(1)} %bitcast.79, f32[64]{0:T(128)S(1)} %add_rsqrt_fusion.2), kind=kOutput, calls=%fused_computation.2 | convolution fusion | flops 1880965120 | bytes 33816832 | tf_op jit(solution)/shard_map/dot_general | solution.py:27
  272.8 6.6 %fusion.8 = f32[64,896]{1,0:T(8,128)S(1)} fusion(bf16[2,8192,896]{2,1,0:T(8,128)(2,1)} %param.7, f32[64,8192]{1,0:T(8,128)S(1)} %copy-done.2, f32[64]{0:T(128)S(1)} %add_rsqrt_fusion, f32[8192]{0:T(1024)S(1)} %bitcast.80), kind=kOutput, calls=%fused_computation.8 | convolution fusion | flops 941096960 | bytes 17039616 | tf_op jit(solution)/shard_map/dot_general | solution.py:24
  279.5 16.4 %fusion = f32[64,8192]{1,0:T(8,128)} fusion(bf16[2,896,8192]{2,1,0:T(8,128)(2,1)} %param.9, bf16[2,8192,896]{2,1,0:T(8,128)(2,1)} %param.8, f32[64,896]{1,0:T(8,128)S(1)} %fusion.8, f32[64,8192]{1,0:T(8,128)S(1)} %copy-done.2, f32[64]{0:T(128)S(1)} %add_rsqrt_fusion, f32[8192]{0:T(1024)S(1)} %bitcast.81), kind=kOutput, calls=%fused_computation | convolution fusion | flops 1880965120 | bytes 33816832 | tf_op jit(solution)/shard_map/dot_general | solution.py:27
  295.8 0.0 all-reduce.5.cloned.1.call-update
  295.9 110.6 %all-reduce.5.cloned.1.call-done = (f32[64,8192]{1,0:T(8,128)}, f32[64,8192]{1,0:T(8,128)}) async-done(((f32[64,8192]{1,0:T(8,128)}, f32[64,8192]{1,0:T(8,128)}), (f32[64,8192]{1,0:T(8,128)}, f32[64,8192]{1,0:T(8,128)})) %all-reduce.5.cloned.1.call-update) | async-done | bytes 4194320 | tf_op jit(solution)/shard_map/psum | solution.py:28
  406.4 1.0 fusion.110
  407.4 0.9 fusion.111
  408.3 0.7 pad_maximum_fusion
  (8 shorter events, 0.0 us)
Async XLA Ops:
  6.5 42.4 %all-gather.5.cloned.1.call-start = ((), (), s32[]{:S(2)}) async-start(), calls=%async_computation | async-start | bytes 1114112 | tf_op jit(solution)/shard_map/all_gather | solution.py:14
  8.1 79.3 %all-gather.7.cloned.1.call-start = ((), (), s32[]{:S(2)}) async-start(), calls=%async_computation.1 | async-start | bytes 1114112 | tf_op jit(solution)/shard_map/all_gather | solution.py:14
  8.8 237.2 %all-reduce.7.cloned.1.call-start = ((), (), s32[]{:S(2)}) async-start(), calls=%async_computation.3 | async-start | bytes 8388608 | tf_op jit(solution)/shard_map/psum | solution.py:28
  48.9 40.0 %copy-start = (bf16[1,64,8192]{2,1,0:T(8,128)(2,1)S(1)}, bf16[1,64,8192]{2,1,0:T(8,128)(2,1)}, u32[]{:S(2)}) copy-start(bf16[1,64,8192]{2,1,0:T(8,128)(2,1)} %all-gather.5.cloned.1.call-done) | copy-start | bytes 3145732
  88.9 6.7 %copy-start.1 = (bf16[1,64,8192]{2,1,0:T(8,128)(2,1)S(1)}, bf16[1,64,8192]{2,1,0:T(8,128)(2,1)}, u32[]{:S(2)}) copy-start(bf16[1,64,8192]{2,1,0:T(8,128)(2,1)} %all-gather.7.cloned.1.call-done) | copy-start | bytes 3145732
  134.9 271.5 %all-reduce.5.cloned.1.call-start = ((), (), s32[]{:S(2)}) async-start(), calls=%async_computation.2 | async-start | bytes 8388608 | tf_op jit(solution)/shard_map/psum | solution.py:28
  250.2 1.4 copy-start.3
  258.2 14.6 %copy-start.2 = (f32[64,8192]{1,0:T(8,128)S(1)}, f32[64,8192]{1,0:T(8,128)}, u32[]{:S(2)}) copy-start(f32[64,8192]{1,0:T(8,128)} %get-tuple-element.12) | copy-start | bytes 6291460
Sparse Core Ops, SparseCore 0:
  9.5 39.3 all-gather.4
  51.0 36.2 all-gather.6
  135.1 110.9 all-reduce.6
  296.0 110.3 all-reduce.4
where the time goes:
time: 416 us
  waiting for transfers between devices  298 us (72%)
  matrix products  90.2 us (22%)
  between operations  13.2 us (3%)
  other arithmetic  9.94 us (2%)
    psum x2, waiting for transfers between devices, body(): branch = lax.psum(partials, 'width')  221 us
    all_gather x2, waiting for transfers between devices, body(): lax.all_gather(stream_in[micro_index], 'width', axis=1, tiled=True)  75.8 us
    dot_general x4, matrix products, body(): jnp.dot(hidden, w_down[depth], preferred_element_type=jnp.float32)  63.7 us
    dot_general x4, matrix products, body(): jnp.dot(normed, w_gate[depth], preferred_element_type=jnp.float32)  26.5 us
  transfers between devices with their start and end apart: 4, of which 4 were waited for; matrix products, arithmetic and copies ran while one was open for 1% of the time, Pallas kernels for 0%

commit v1 on v0

v1 whole, which is shorter than its diff:
```python
import functools

import jax
import jax.numpy as jnp
from jax import lax
from jax.experimental import pallas as pl
from jax.experimental.pallas import tpu as pltpu
from jax.sharding import PartitionSpec as P

MESH = pl.DeviceIdType.MESH


def plain_body(stream_in, norm_gain, w_gate, w_up, w_down):
    micro, rows, own_width = stream_in.shape
    stream = stream_in.reshape(micro * rows, own_width)
    for depth in range(w_gate.shape[0]):
        whole = lax.all_gather(stream, "width", axis=1, tiled=True).astype(jnp.float32)
        meansq = jnp.mean(whole * whole, axis=1, keepdims=True)
        normed = (whole * lax.rsqrt(meansq + 1e-05) * norm_gain[depth]).astype(jnp.bfloat16)
        gate_out = jnp.dot(normed, w_gate[depth], preferred_element_type=jnp.float32)
        up_out = jnp.dot(normed, w_up[depth], preferred_element_type=jnp.float32)
        hidden = (jax.nn.silu(gate_out) * up_out).astype(jnp.bfloat16)
        partials = jnp.dot(hidden, w_down[depth], preferred_element_type=jnp.float32)
        branch = lax.psum_scatter(partials, "width", scatter_dimension=1, tiled=True)
        stream = (stream.astype(jnp.float32) + branch).astype(jnp.bfloat16)
    return stream.reshape(micro, rows, own_width)


def solution(mesh):
    return jax.shard_map(
        plain_body,
        mesh=mesh,
        in_specs=(
            P(None, "groups", "width"),
            P(),
            P(None, None, "width"),
            P(None, None, "width"),
            P(None, "width", None),
        ),
        out_specs=P(None, "groups", "width"),
        check_vma=False,
    )
```

time: 416 us -> 297 us (0.71)
  waiting for transfers between devices: 298 us -> 230 us
  matrix products: 90.2 us -> 44.4 us
    psum x2 -> x0, waiting for transfers between devices: 221 us -> none  [body(): branch = lax.psum(partials, 'width')]
    reduce_scatter x0 -> x2, waiting for transfers between devices: none -> 144 us  [plain_body(): lax.psum_scatter(partials, 'width', scatter_dimension=1, tiled=True)]
    dot_general x8 -> x4, matrix products: 90.2 us -> 44.4 us  [the longest x2 27.8 us: plain_body(): jnp.dot(hidden, w_down[depth], preferred_element_type=jnp.float32)]
    all_gather x2, waiting for transfers between devices: 75.8 us -> 85.5 us  [plain_body(): lax.all_gather(stream, 'width', axis=1, tiled=True).astype(jnp.float32)]
  transfers between devices with their start and end apart: 4 -> 4, of which waited for: 4 -> 4; matrix products, arithmetic and copies ran while one was open for 1% -> 0% of each run, Pallas kernels for 0% -> 0%
where the time goes in v1:
time: 297 us
  waiting for transfers between devices  230 us (77%)
  matrix products  44.4 us (15%)
  between operations  13.2 us (4%)
  other arithmetic  7.43 us (3%)
    reduce_scatter x2, waiting for transfers between devices, plain_body(): lax.psum_scatter(partials, 'width', scatter_dimension=1, tiled=True)  144 us
    all_gather x2, waiting for transfers between devices, plain_body(): lax.all_gather(stream, 'width', axis=1, tiled=True).astype(jnp.float32)  85.5 us
    dot_general x2, matrix products, plain_body(): jnp.dot(hidden, w_down[depth], preferred_element_type=jnp.float32)  27.8 us
    dot_general x2, matrix products, plain_body(): jnp.dot(normed, w_gate[depth], preferred_element_type=jnp.float32)  16.7 us
  transfers between devices with their start and end apart: 4, of which 4 were waited for; matrix products, arithmetic and copies ran while one was open for 0% of the time, Pallas kernels for 0%

profile of v1, /device:TPU:0, one launch (start us, length us, event | category | flops | bytes accessed | tf_op | source)
XLA Modules:
  0.0 296.5 jit_solution(17220624343534082053)
XLA Ops:
  6.5 0.0 all-gather.3.cloned.1.call-start
  6.5 0.7 all-gather.3.cloned.1.call-update
  7.3 0.0 reduce-scatter.3.cloned.1.call-start
  7.3 1.0 fusion.62
  8.3 45.0 %all-gather.3.cloned.1.call-done = bf16[128,8192]{1,0:T(8,128)(2,1)} async-done(((bf16[128,512]{1,0:T(8,128)(2,1)}), bf16[128,8192]{1,0:T(8,128)(2,1)}) %all-gather.3.cloned.1.call-update) | async-done | bytes 2097168 | tf_op jit(solution)/shard_map/all_gather | solution.py:17
  53.3 2.1 fusion.18
  55.4 0.0 copy-start
  55.4 8.3 %fusion.10 = f32[128,896]{1,0:T(8,128)S(1)} fusion(bf16[2,8192,896]{2,1,0:T(8,128)(2,1)} %param.7, bf16[128,8192]{1,0:T(8,128)(2,1)} %all-gather.3.cloned.1.call-done, f32[8192]{0:T(1024)S(1)} %bitcast.38, f32[128]{0:T(128)S(1)} %add_rsqrt_fusion.1), kind=kOutput, calls=%fused_computation.10 | convolution fusion | flops 1883242496 | bytes 17269248 | tf_op jit(solution)/shard_map/dot_general | solution.py:20
  63.7 0.0 copy-done
  63.7 13.9 %fusion.6 = f32[128,8192]{1,0:T(8,128)} fusion(bf16[2,896,8192]{2,1,0:T(8,128)(2,1)} %param.9, bf16[2,8192,896]{2,1,0:T(8,128)(2,1)} %param.8, bf16[128,8192]{1,0:T(8,128)(2,1)S(1)} %copy-done, f32[8192]{0:T(1024)S(1)} %bitcast.39, f32[128]{0:T(128)S(1)} %add_rsqrt_fusion.1, f32[128,896]{1,0:T(8,128)S(1)} %fusion.10), kind=kOutput, calls=%fused_computation.6 | convolution fusion | flops 3762978816 | bytes 36143616 | tf_op jit(solution)/shard_map/dot_general | solution.py:23
  77.6 0.0 copy-start.3
  77.6 0.0 reduce-scatter.3.cloned.1.call-update
  77.6 0.0 all-gather.5.cloned.1.call-start
  77.7 72.0 %reduce-scatter.3.cloned.1.call-done = f32[128,512]{1,0:T(8,128)} async-done(((f32[128,8192]{1,0:T(8,128)}), f32[128,512]{1,0:T(8,128)}) %reduce-scatter.3.cloned.1.call-update) | async-done | bytes 262160 | tf_op jit(solution)/shard_map/reduce_scatter | solution.py:24
  149.7 0.0 copy-done.3
  149.7 1.6 add_convert_fusion.1
  151.4 0.0 all-gather.5.cloned.1.call-update
  151.4 0.0 reduce-scatter.5.cloned.1.call-start
  151.4 40.5 %all-gather.5.cloned.1.call-done = bf16[128,8192]{1,0:T(8,128)(2,1)} async-done(((bf16[128,512]{1,0:T(8,128)(2,1)}), bf16[128,8192]{1,0:T(8,128)(2,1)}) %all-gather.5.cloned.1.call-update) | async-done | bytes 2097168 | tf_op jit(solution)/shard_map/all_gather | solution.py:17
  192.0 2.1 fusion.21
  194.1 0.0 copy-start.1
  194.1 8.3 %fusion.4 = f32[128,896]{1,0:T(8,128)S(1)} fusion(bf16[2,8192,896]{2,1,0:T(8,128)(2,1)} %param.7, bf16[128,8192]{1,0:T(8,128)(2,1)} %all-gather.5.cloned.1.call-done, f32[8192]{0:T(1024)S(1)} %bitcast.36, f32[128]{0:T(128)S(1)} %add_rsqrt_fusion), kind=kOutput, calls=%fused_computation.4 | convolution fusion | flops 1883242496 | bytes 17269248 | tf_op jit(solution)/shard_map/dot_general | solution.py:20
  202.4 0.0 copy-done.1
  202.4 13.9 %fusion = f32[128,8192]{1,0:T(8,128)} fusion(bf16[2,896,8192]{2,1,0:T(8,128)(2,1)} %param.9, bf16[2,8192,896]{2,1,0:T(8,128)(2,1)} %param.8, bf16[128,8192]{1,0:T(8,128)(2,1)S(1)} %copy-done.1, f32[8192]{0:T(1024)S(1)} %bitcast.37, f32[128]{0:T(128)S(1)} %add_rsqrt_fusion, f32[128,896]{1,0:T(8,128)S(1)} %fusion.4), kind=kOutput, calls=%fused_computation | convolution fusion | flops 3762978816 | bytes 36143616 | tf_op jit(solution)/shard_map/dot_general | solution.py:23
  216.3 0.0 copy-start.2
  216.3 0.0 reduce-scatter.5.cloned.1.call-update
  216.3 72.1 %reduce-scatter.5.cloned.1.call-done = f32[128,512]{1,0:T(8,128)} async-done(((f32[128,8192]{1,0:T(8,128)}), f32[128,512]{1,0:T(8,128)}) %reduce-scatter.5.cloned.1.call-update) | async-done | bytes 262160 | tf_op jit(solution)/shard_map/reduce_scatter | solution.py:24
  288.4 0.0 copy-done.2
  288.4 1.6 add_convert_fusion
  (2 shorter events, 0.0 us)
Async XLA Ops:
  6.5 46.7 %all-gather.3.cloned.1.call-start = ((), (), s32[]{:S(2)}) async-start(), calls=%async_computation.2 | async-start | bytes 2228224 | tf_op jit(solution)/shard_map/all_gather | solution.py:17
  7.3 142.5 %reduce-scatter.3.cloned.1.call-start = ((), (), s32[]{:S(2)}) async-start(), calls=%async_computation.3 | async-start | bytes 4456448 | tf_op jit(solution)/shard_map/reduce_scatter | solution.py:24
  55.4 8.4 %copy-start = (bf16[128,8192]{1,0:T(8,128)(2,1)S(1)}, bf16[128,8192]{1,0:T(8,128)(2,1)}, u32[]{:S(2)}) copy-start(bf16[128,8192]{1,0:T(8,128)(2,1)} %all-gather.3.cloned.1.call-done) | copy-start | bytes 6291460
  77.6 72.1 %copy-start.3 = (bf16[2,64,512]{2,1,0:T(8,128)(2,1)S(1)}, bf16[2,64,512]{2,1,0:T(8,128)(2,1)}, u32[]{:S(2)}) copy-start(bf16[2,64,512]{2,1,0:T(8,128)(2,1)} %param.5) | copy-start | bytes 393220
  77.6 114.3 %all-gather.5.cloned.1.call-start = ((), (), s32[]{:S(2)}) async-start(), calls=%async_computation.4 | async-start | bytes 2228224 | tf_op jit(solution)/shard_map/all_gather | solution.py:17
  151.4 137.0 %reduce-scatter.5.cloned.1.call-start = ((), (), s32[]{:S(2)}) async-start(), calls=%async_computation.5 | async-start | bytes 4456448 | tf_op jit(solution)/shard_map/reduce_scatter | solution.py:24
  194.1 8.4 %copy-start.1 = (bf16[128,8192]{1,0:T(8,128)(2,1)S(1)}, bf16[128,8192]{1,0:T(8,128)(2,1)}, u32[]{:S(2)}) copy-start(bf16[128,8192]{1,0:T(8,128)(2,1)} %all-gather.5.cloned.1.call-done) | copy-start | bytes 6291460
  216.3 72.1 %copy-start.2 = (bf16[128,512]{1,0:T(8,128)(2,1)S(1)}, bf16[128,512]{1,0:T(8,128)(2,1)}, u32[]{:S(2)}) copy-start(bf16[128,512]{1,0:T(8,128)(2,1)} %add_convert_fusion.1) | copy-start | bytes 393220
Sparse Core Ops, SparseCore 0:
  9.5 43.7 all-gather.2
  77.8 71.9 reduce-scatter.2
  151.9 40.0 all-gather.4
  216.4 71.8 reduce-scatter.4

commit v2 on v1

--- a/solution.py
+++ b/solution.py
@@ -26,9 +26,264 @@
     return stream.reshape(micro, rows, own_width)
 
 
+def kernel(
+    n, x_ref, gain_ref, wg_ref, wu_ref, wd_ref, out_ref,
+    pair_w, down_w, parts, scaled, acc, squares, hidden, own,
+    core_out, core_in, y_out, y_in, z_out, z_in, keep,
+    pair_sem, down_sem, gather_send, gather_recv, sum_send, core_recv, y_recv, z_recv,
+):
+    layers = wg_ref.shape[0]
+    chips, nz = n // 2, n // 4
+    width = x_ref.shape[1]
+    chunk = 2 * width
+    me = lax.axis_index("width")
+    c, y, z = lax.rem(me, 2), lax.rem(me // 2, 2), me // 4
+
+    def device(zi, yi, ci):
+        return (zi * 2 + yi) * 2 + ci
+
+    core_peer, y_peer = device(z, y, 1 - c), device(z, 1 - y, c)
+
+    def turn(step):
+        return lax.rem(z + step, nz)
+
+    def pair_copy(depth, chip, j):
+        src = wg_ref if j == 0 else wu_ref
+        rows = pl.ds(pl.multiple_of(chip * chunk, chunk), chunk)
+        return pltpu.make_async_copy(src.at[depth, rows, :], pair_w.at[chip, j], pair_sem.at[chip, j])
+
+    def down_copy(depth, dev):
+        cols = pl.ds(pl.multiple_of(dev * width, width), width)
+        return pltpu.make_async_copy(wd_ref.at[depth, :, cols], down_w.at[dev], down_sem.at[dev])
+
+    def remote(src, dst, send, recv, dev):
+        return pltpu.make_async_remote_copy(
+            src_ref=src, dst_ref=dst, send_sem=send, recv_sem=recv,
+            device_id={"width": dev}, device_id_type=MESH,
+        )
+
+    def load_pairs(chip):
+        pair_copy(0, chip, 0).start()
+        pair_copy(0, chip, 1).start()
+
+    load_pairs(z * 2 + y)
+
+    barrier = pltpu.get_barrier_semaphore()
+    peers = [core_peer, y_peer] + [device(turn(j), y, c) for j in range(1, nz)]
+    for peer in peers:
+        pl.semaphore_signal(barrier, inc=1, device_id={"width": peer}, device_id_type=MESH)
+
+    for k in range(1, nz):
+        load_pairs(turn(k) * 2 + y)
+        load_pairs(turn(k - 1) * 2 + 1 - y)
+    load_pairs(turn(nz - 1) * 2 + 1 - y)
+
+    def down_chip(t):
+        return turn(lax.rem(t, nz) + 1) * 2 + jnp.where(t < nz, 1 - y, y)
+
+    @pl.loop(0, chips)
+    def _(t):
+        chip = down_chip(t)
+        down_copy(0, chip * 2 + 1 - c).start()
+        down_copy(0, chip * 2 + c).start()
+
+    pl.semaphore_wait(barrier, len(peers))
+
+    for depth in range(layers):
+        mine = x_ref if depth == 0 else own.at[depth]
+
+        def to_peer(src, owner, slot, dev):
+            return remote(src, parts.at[depth, owner], gather_send.at[depth, slot], gather_recv.at[depth, owner], dev)
+
+        def arrived(owner):
+            to_peer(mine, owner, 0, core_peer).wait_recv()
+
+        to_peer(mine, me, nz - 1, y_peer).start()
+        for j in range(1, nz):
+            to_peer(mine, me, j - 1, device(turn(nz - j), y, c)).start()
+        to_peer(mine, me, 2 * nz - 1, core_peer).start()
+        parts[depth, me] = mine[...]
+        acc[...] = jnp.zeros_like(acc)
+        squares[...] = jnp.zeros_like(squares)
+
+        def gate_up(chip):
+            for h in range(2):
+                piece = parts[depth, chip * 2 + h].astype(jnp.float32)
+                cols = pl.ds(pl.multiple_of((chip * 2 + h) * width, width), width)
+                scaled[:, h * width:(h + 1) * width] = (piece * gain_ref[depth:depth + 1, cols]).astype(jnp.bfloat16)
+                sq = piece * piece
+                total = sq[:, :128]
+                for i in range(1, width // 128):
+                    total = total + sq[:, i * 128:(i + 1) * 128]
+                squares[...] += total
+            for j in range(2):
+                pair_copy(depth, chip, j).wait()
+
+            @pl.loop(0, 2)
+            def _(j):
+                acc[j] += jnp.dot(scaled[...], pair_w[chip, j], preferred_element_type=jnp.float32)
+
+            if depth + 1 < layers:
+                for j in range(2):
+                    pair_copy(depth + 1, chip, j).start()
+
+        @pl.loop(0, nz + 1)
+        def _(k):
+            @pl.when(k < nz)
+            def _():
+                chip = turn(k) * 2 + y
+                arrived(chip * 2 + 1 - c)
+                gate_up(chip)
+
+            @pl.when(k + 1 < nz)
+            def _():
+                owner = device(turn(k + 1), y, c)
+                arrived(owner)
+                to_peer(parts.at[depth, owner], owner, nz + k, y_peer).start()
+                to_peer(parts.at[depth, owner], owner, 2 * nz + k, core_peer).start()
+
+            @pl.when(k < nz)
+            def _():
+                owner = device(turn(k), 1 - y, c)
+                arrived(owner)
+                to_peer(parts.at[depth, owner], owner, 3 * nz - 1 + k, core_peer).start()
+
+            @pl.when(k > 0)
+            def _():
+                chip = turn(k - 1) * 2 + 1 - y
+                arrived(chip * 2 + 1 - c)
+                gate_up(chip)
+
+        meansq = jnp.sum(squares[...], axis=1, keepdims=True) / (n * width)
+        scale = lax.rsqrt(meansq + 1e-05)
+        gate_out = acc[0] * scale
+        hidden[...] = (gate_out / (1.0 + jnp.exp(-gate_out)) * (acc[1] * scale)).astype(jnp.bfloat16)
+
+        def core_copy(chip):
+            return remote(core_out.at[depth, chip], core_in.at[depth, chip],
+                          sum_send.at[depth, chip], core_recv.at[depth, chip], core_peer)
+
+        def y_copy(zi):
+            return remote(y_out.at[depth, zi], y_in.at[depth, zi],
+                          sum_send.at[depth, chips + zi], y_recv.at[depth, zi], y_peer)
+
+        def z_copy(zi, slot):
+            return remote(z_out.at[depth, zi], z_in.at[depth, slot],
+                          sum_send.at[depth, chips + nz + zi], z_recv.at[depth, slot], device(zi, y, c))
+
+        def down(dev):
+            down_copy(depth, dev).wait()
+            return jnp.dot(hidden[...], down_w[dev], preferred_element_type=jnp.float32)
+
+        @pl.loop(0, chips)
+        def _(t):
+            chip = down_chip(t)
+            core_out[depth, chip] = down(chip * 2 + 1 - c).astype(jnp.bfloat16)
+            core_copy(chip).start()
+            keep[chip] = down(chip * 2 + c)
+            if depth + 1 < layers:
+                down_copy(depth + 1, chip * 2 + 1 - c).start()
+                down_copy(depth + 1, chip * 2 + c).start()
+
+            @pl.when((t > 0) & (t <= nz))
+            def _():
+                zi = turn(t)
+                far = zi * 2 + 1 - y
+                core_copy(far).wait_recv()
+                y_out[depth, zi] = (keep[far] + core_in[depth, far].astype(jnp.float32)).astype(jnp.bfloat16)
+                y_copy(zi).start()
+
+        def near(zi):
+            chip = zi * 2 + y
+            core_copy(chip).wait_recv()
+            total = keep[chip] + core_in[depth, chip].astype(jnp.float32)
+            y_copy(zi).wait_recv()
+            return total + y_in[depth, zi].astype(jnp.float32)
+
+        @pl.loop(1, nz)
+        def _(k):
+            zi = turn(k)
+            z_out[depth, zi] = near(zi).astype(jnp.bfloat16)
+            z_copy(zi, z).start()
+
+        total = near(z) + mine[...].astype(jnp.float32)
+        for k in range(1, nz):
+            zi = turn(k)
+            z_copy(zi, zi).wait_recv()
+            total = total + z_in[depth, zi].astype(jnp.float32)
+        if depth + 1 < layers:
+            own[depth + 1] = total.astype(jnp.bfloat16)
+        else:
+            out_ref[...] = total.astype(jnp.bfloat16)
+
+    for depth in range(layers):
+        @pl.loop(0, n - 1)
+        def _(i):
+            remote(x_ref, parts.at[depth, me], gather_send.at[depth, i], gather_recv.at[depth, me], core_peer).wait_send()
+
+        @pl.loop(0, chips + nz)
+        def _(i):
+            remote(x_ref, parts.at[depth, me], sum_send.at[depth, i], gather_recv.at[depth, me], core_peer).wait_send()
+
+        for k in range(1, nz):
+            remote(x_ref, parts.at[depth, me], sum_send.at[depth, chips + nz + turn(k)], gather_recv.at[depth, me], core_peer).wait_send()
+
+
+def fused(n, stream_in, norm_gain, w_gate, w_up, w_down):
+    micro, rows, width = stream_in.shape
+    layers, d, ff = w_gate.shape
+    m, chips, nz = micro * rows, n // 2, n // 4
+    bf, f32, dma = jnp.bfloat16, jnp.float32, pltpu.SemaphoreType.DMA
+    vmem = pl.BlockSpec(memory_space=pltpu.VMEM)
+    hbm = pl.BlockSpec(memory_space=pltpu.HBM)
+    out = pl.pallas_call(
+        functools.partial(kernel, n),
+        out_shape=jax.ShapeDtypeStruct((m, width), bf),
+        in_specs=[vmem, vmem, hbm, hbm, hbm],
+        out_specs=vmem,
+        scratch_shapes=[
+            pltpu.VMEM((chips, 2, 2 * width, ff), bf),
+            pltpu.VMEM((n, ff, width), bf),
+            pltpu.VMEM((layers, n, m, width), bf),
+            pltpu.VMEM((m, 2 * width), bf),
+            pltpu.VMEM((2, m, ff), f32),
+            pltpu.VMEM((m, 128), f32),
+            pltpu.VMEM((m, ff), bf),
+            pltpu.VMEM((layers, m, width), bf),
+            pltpu.VMEM((layers, chips, m, width), bf),
+            pltpu.VMEM((layers, chips, m, width), bf),
+            pltpu.VMEM((layers, nz, m, width), bf),
+            pltpu.VMEM((layers, nz, m, width), bf),
+            pltpu.VMEM((layers, nz, m, width), bf),
+            pltpu.VMEM((layers, nz, m, width), bf),
+            pltpu.VMEM((chips, m, width), f32),
+            dma((chips, 2)),
+            dma((n,)),
+            dma((layers, n - 1)),
+            dma((layers, n)),
+            dma((layers, chips + 2 * nz)),
+            dma((layers, chips)),
+            dma((layers, nz)),
+            dma((layers, nz)),
+        ],
+        compiler_params=pltpu.CompilerParams(
+            collective_id=0, has_side_effects=True, vmem_limit_bytes=67_043_328
+        ),
+    )(stream_in.reshape(m, width), norm_gain, w_gate, w_up, w_down)
+    return out.reshape(micro, rows, width)
+
+
+def body(n, stream_in, norm_gain, w_gate, w_up, w_down):
+    aligned = stream_in.shape[2] % 128 == 0 and w_gate.shape[2] % 128 == 0 and n % 4 == 0
+    held = w_gate[0].size * 6
+    if aligned and n > 4 and held < 48 * 2**20:
+        return fused(n, stream_in, norm_gain, w_gate, w_up, w_down)
+    return plain_body(stream_in, norm_gain, w_gate, w_up, w_down)
+
+
 def solution(mesh):
     return jax.shard_map(
-        plain_body,
+        functools.partial(body, mesh.shape["width"]),
         mesh=mesh,
         in_specs=(
             P(None, "groups", "width"),

time: 297 us -> 90 us (0.30)
  waiting for transfers between devices: 230 us -> 0 us
  Pallas kernels: 0 us -> 88.3 us
  matrix products: 44.4 us -> 0 us
  between operations: 13.2 us -> 0.01 us
  other arithmetic: 7.43 us -> 0 us
    reduce_scatter x2 -> x0, waiting for transfers between devices: 144 us -> none  [plain_body(): lax.psum_scatter(partials, 'width', scatter_dimension=1, tiled=True)]
    pallas_call x0 -> x1, Pallas kernels: none -> 88.3 us  [fused(): pl.pallas_call(functools.partial(kernel, n), out_shape=jax.ShapeDtypeStru...]
    all_gather x2 -> x0, waiting for transfers between devices: 85.5 us -> none  [plain_body(): lax.all_gather(stream, 'width', axis=1, tiled=True).astype(jnp.float32)]
    dot_general x4 -> x0, matrix products: 44.4 us -> none  [the longest x2 27.8 us: plain_body(): jnp.dot(hidden, w_down[depth], preferred_element_type=jnp.float32)]
    reduce_sum x2 -> x0, other arithmetic: 4.15 us -> none  [plain_body(): meansq = jnp.mean(whole * whole, axis=1, keepdims=True)]
    convert_element_type x2 -> x0, other arithmetic: 3.26 us -> none  [plain_body(): stream = (stream.astype(jnp.float32) + branch).astype(jnp.bfloat16)]
  transfers between devices with their start and end apart: 4 -> 0, of which waited for: 4 -> 0; matrix products, arithmetic and copies ran while one was open for 0% -> 0% of each run, Pallas kernels for 0% -> 0%
where the time goes in v2:
time: 90 us; the launch traced here: 89.9 us
  Pallas kernels  88.3 us (98%)
  local copies, waits for them, and re-layouts  1.57 us (2%)
    pallas_call x1, Pallas kernels, fused(): pl.pallas_call(functools.partial(kernel, n), out_shape=jax.ShapeDtypeStru...  88.3 us

profile of v2, /device:TPU:0, one launch (start us, length us, event | category | flops | bytes accessed | tf_op | source)
XLA Modules:
  0.0 89.9 jit_solution(12479002838256406264)
XLA Ops:
  0.0 88.3 %shard_map.55 = bf16[128,512]{1,0:T(8,128)(2,1)} custom-call(bf16[128,512]{1,0:T(8,128)(2,1)} %bitcast.3, f32[2,8192]{1,0:T(2,128)} %gain_ref.1, bf16[2,8192,896]{2,1,0:T(8,128)(2,1)} %wg_ref.1, bf16[2,8192,896]{2,1,0:T(8,128)(2,1)} %wu_ref.1, bf16[2,896,8192]{2,1,0:T(8,128)(2,1)} %wd_ref.1), custom_call_target="tpu_custom_call" | custom-call | tf_op jit(solution)/shard_map/pallas_call | solution.py:239
  88.3 1.6 %copy.7 = bf16[2,64,512]{2,1,0:T(8,128)(2,1)} copy(bf16[2,64,512]{2,1,0:T(8,128)(2,1)} %bitcast.2) | data formatting | bytes 262144

commit v3 on v2

--- a/solution.py
+++ b/solution.py
@@ -47,6 +47,12 @@
     def turn(step):
         return lax.rem(z + step, nz)
 
+    low = z < nz // 2
+
+    def order(k):
+        rank = k - 1 + jnp.where(k - 1 >= jnp.where(low, z, nz - 1 - z), 1, 0)
+        return jnp.where(k == 0, z, jnp.where(low, rank, nz - 1 - rank))
+
     def pair_copy(depth, chip, j):
         src = wg_ref if j == 0 else wu_ref
         rows = pl.ds(pl.multiple_of(chip * chunk, chunk), chunk)
@@ -74,9 +80,9 @@
         pl.semaphore_signal(barrier, inc=1, device_id={"width": peer}, device_id_type=MESH)
 
     for k in range(1, nz):
-        load_pairs(turn(k) * 2 + y)
-        load_pairs(turn(k - 1) * 2 + 1 - y)
-    load_pairs(turn(nz - 1) * 2 + 1 - y)
+        load_pairs(order(k) * 2 + y)
+        load_pairs(order(k - 1) * 2 + 1 - y)
+    load_pairs(order(nz - 1) * 2 + 1 - y)
 
     def down_chip(t):
         return turn(lax.rem(t, nz) + 1) * 2 + jnp.where(t < nz, 1 - y, y)
@@ -99,8 +105,15 @@
             to_peer(mine, owner, 0, core_peer).wait_recv()
 
         to_peer(mine, me, nz - 1, y_peer).start()
-        for j in range(1, nz):
-            to_peer(mine, me, j - 1, device(turn(nz - j), y, c)).start()
+
+        @pl.when(z < nz - 1)
+        def _():
+            to_peer(mine, me, n - 1 + z, device(z + 1, y, c)).start()
+
+        @pl.when(z > 0)
+        def _():
+            to_peer(mine, me, n - 1 + nz, device(z - 1, y, c)).start()
+
         to_peer(mine, me, 2 * nz - 1, core_peer).start()
         parts[depth, me] = mine[...]
         acc[...] = jnp.zeros_like(acc)
@@ -131,26 +144,36 @@
         def _(k):
             @pl.when(k < nz)
             def _():
-                chip = turn(k) * 2 + y
+                chip = order(k) * 2 + y
                 arrived(chip * 2 + 1 - c)
                 gate_up(chip)
 
             @pl.when(k + 1 < nz)
             def _():
-                owner = device(turn(k + 1), y, c)
+                zi = order(k + 1)
+                owner = device(zi, y, c)
                 arrived(owner)
+
+                @pl.when((zi < z) & (z < nz - 1))
+                def _():
+                    to_peer(parts.at[depth, owner], owner, n - 1 + zi, device(z + 1, y, c)).start()
+
+                @pl.when((zi > z) & (z > 0))
+                def _():
+                    to_peer(parts.at[depth, owner], owner, n - 1 + zi, device(z - 1, y, c)).start()
+
                 to_peer(parts.at[depth, owner], owner, nz + k, y_peer).start()
                 to_peer(parts.at[depth, owner], owner, 2 * nz + k, core_peer).start()
 
             @pl.when(k < nz)
             def _():
-                owner = device(turn(k), 1 - y, c)
+                owner = device(order(k), 1 - y, c)
                 arrived(owner)
                 to_peer(parts.at[depth, owner], owner, 3 * nz - 1 + k, core_peer).start()
 
             @pl.when(k > 0)
             def _():
-                chip = turn(k - 1) * 2 + 1 - y
+                chip = order(k - 1) * 2 + 1 - y
                 arrived(chip * 2 + 1 - c)
                 gate_up(chip)
 
@@ -217,7 +240,20 @@
             out_ref[...] = total.astype(jnp.bfloat16)
 
     for depth in range(layers):
-        @pl.loop(0, n - 1)
+        def gather_sent(i):
+            remote(x_ref, parts.at[depth, me], gather_send.at[depth, i], gather_recv.at[depth, me], core_peer).wait_send()
+
+        @pl.loop(0, nz)
+        def _(zi):
+            @pl.when(((zi <= z) & (z < nz - 1)) | ((zi > z) & (z > 0)))
+            def _():
+                gather_sent(n - 1 + zi)
+
+        @pl.when(z > 0)
+        def _():
+            gather_sent(n - 1 + nz)
+
+        @pl.loop(nz - 1, n - 1)
         def _(i):
             remote(x_ref, parts.at[depth, me], gather_send.at[depth, i], gather_recv.at[depth, me], core_peer).wait_send()
 
@@ -259,7 +295,7 @@
             pltpu.VMEM((chips, m, width), f32),
             dma((chips, 2)),
             dma((n,)),
-            dma((layers, n - 1)),
+            dma((layers, n + nz)),
             dma((layers, n)),
             dma((layers, chips + 2 * nz)),
             dma((layers, chips)),

time: 90 us -> 85.7 us (0.952)
  Pallas kernels: 88.3 us -> 84 us
    pallas_call x1, Pallas kernels: 88.3 us -> 84 us  [fused(): pl.pallas_call(functools.partial(kernel, n), out_shape=jax.ShapeDtypeStru...]
where the time goes in v3:
time: 85.7 us; the launch traced here: 85.5 us
  Pallas kernels  84 us (98%)
  local copies, waits for them, and re-layouts  1.57 us (2%)
    pallas_call x1, Pallas kernels, fused(): pl.pallas_call(functools.partial(kernel, n), out_shape=jax.ShapeDtypeStru...  84 us

profile of v3, /device:TPU:0, one launch (start us, length us, event | category | flops | bytes accessed | tf_op | source)
XLA Modules:
  0.0 85.5 jit_solution(6678174227018447354)
XLA Ops:
  0.0 84.0 %shard_map.55 = bf16[128,512]{1,0:T(8,128)(2,1)} custom-call(bf16[128,512]{1,0:T(8,128)(2,1)} %bitcast.3, f32[2,8192]{1,0:T(2,128)} %gain_ref.1, bf16[2,8192,896]{2,1,0:T(8,128)(2,1)} %wg_ref.1, bf16[2,8192,896]{2,1,0:T(8,128)(2,1)} %wu_ref.1, bf16[2,896,8192]{2,1,0:T(8,128)(2,1)} %wd_ref.1), custom_call_target="tpu_custom_call" | custom-call | tf_op jit(solution)/shard_map/pallas_call | solution.py:275
  84.0 1.6 %copy.7 = bf16[2,64,512]{2,1,0:T(8,128)(2,1)} copy(bf16[2,64,512]{2,1,0:T(8,128)(2,1)} %bitcast.2) | data formatting | bytes 262144
